TPU v7x, 512 devices: a whole 4x8x8 slice. The times are simulated.
512 devices in a mesh: dp: 4 (over x_lo, core), blk: 128 (over y, z, x_hi).
Axes of the slice: x: 4 (x_hi: 2, x_lo: 2; x = x_hi * 2 + x_lo), y: 8, z: 8, core: 2. Of those that a mesh axis runs over, the one named last changes fastest.
Arguments:
- queries: bfloat16 [4, 24576, 512], P('dp', 'blk'), may hold values from -6 to 6, as said below
- key_in: bfloat16 [4, 24576, 512], P('dp', 'blk'), may hold values from -6 to 6, as said below
- value_in: bfloat16 [4, 24576, 512], P('dp', 'blk'), may hold values from -6 to 6
- out_weight: bfloat16 [512, 1024], replicated, may hold values from -2 to 2
- conv_kernel: float32 [31, 1024], replicated, may hold values from -1 to 1
- cotangent: bfloat16 [4, 24576, 1024], P('dp', 'blk'), may hold values from -6 to 6
Outputs:
- out_frames: bfloat16 [4, 24576, 1024], P('dp', 'blk')
- query_grad: bfloat16 [4, 24576, 512], P('dp', 'blk')
- key_grad: bfloat16 [4, 24576, 512], P('dp', 'blk')
- value_grad: bfloat16 [4, 24576, 512], P('dp', 'blk')
- weight_grad: float32 [512, 1024], replicated
- kernel_grad: float32 [31, 1024], replicated
Inputs may be any that keep to these rules, and one draw needn't show every extreme that they name: `queries`: independent entries. `key_in`: independent entries.
All inputs are finite; a program needn't handle non-finite values.
Results may differ from a plain program's by a relative error of at most 0.024.
Values may be sent and summed in bfloat16 or wider, within the bound.
A program may use at most 64 MiB of HBM per device.

v0:
```python
import math
import jax
import jax.numpy as jnp
from jax import lax
from jax.sharding import PartitionSpec as P

ATT_HEADS = 8
HEAD_DIM = 64
CTX_MAX = 3
ATT = 512
NEGATIVE = -1e30


def from_behind(block, axis, distance):
    devices = range(lax.axis_size(axis))
    route = [(i - distance, i) for i in devices if i - distance in devices]
    return lax.ppermute(block, axis, route)


def split_heads(matrix):
    return matrix.reshape(matrix.shape[0], ATT_HEADS, HEAD_DIM)


def tile_scores(query_heads, tile, query_pos, key_pos, usable, left_span, score_scale):
    key_heads = split_heads(tile[:, :ATT])
    scores = (
        jnp.einsum("qhd,khd->hqk", query_heads, key_heads, preferred_element_type=jnp.float32)
        * score_scale
    )
    distance = query_pos[:, None] - key_pos[None, :]
    visible = ((distance >= 0) & (distance < left_span) & usable)[None]
    return (jnp.where(visible, scores, NEGATIVE), visible)


def attend_tile(
    softmax_state, query_heads, tile, query_pos, key_pos, usable, left_span, score_scale
):
    running_max, running_sum, weighted = softmax_state
    scores, visible = tile_scores(
        query_heads, tile, query_pos, key_pos, usable, left_span, score_scale
    )
    new_max = jnp.maximum(running_max, jnp.max(scores, axis=-1))
    weights = jnp.where(visible, jnp.exp(scores - new_max[..., None]), 0.0)
    fading = jnp.exp(running_max - new_max)
    running_sum = running_sum * fading + jnp.sum(weights, axis=-1)
    value_heads = split_heads(tile[:, ATT:])
    update = jnp.einsum(
        "hqk,khd->qhd",
        weights.astype(jnp.bfloat16),
        value_heads,
        preferred_element_type=jnp.float32,
    )
    weighted = weighted * jnp.transpose(fading)[:, :, None] + update
    return (new_max, running_sum, weighted)


def tile_grads(
    query_heads,
    dout_heads,
    log_sums,
    deltas,
    tile,
    query_pos,
    key_pos,
    usable,
    left_span,
    score_scale,
):
    scores, visible = tile_scores(
        query_heads, tile, query_pos, key_pos, usable, left_span, score_scale
    )
    key_heads = split_heads(tile[:, :ATT])
    value_heads = split_heads(tile[:, ATT:])
    probs = jnp.where(visible, jnp.exp(scores - log_sums[..., None]), 0.0)
    dvalue_heads = jnp.einsum(
        "hqk,qhd->khd", probs.astype(jnp.bfloat16), dout_heads, preferred_element_type=jnp.float32
    )
    dprobs = jnp.einsum("qhd,khd->hqk", dout_heads, value_heads, preferred_element_type=jnp.float32)
    dscores = (probs * (dprobs - deltas[..., None])).astype(jnp.bfloat16)
    dquery = (
        jnp.einsum("hqk,khd->qhd", dscores, key_heads, preferred_element_type=jnp.float32)
        * score_scale
    )
    dkey_heads = (
        jnp.einsum("hqk,qhd->khd", dscores, query_heads, preferred_element_type=jnp.float32)
        * score_scale
    )
    row_count = tile.shape[0]
    return (
        dquery,
        jnp.concatenate(
            [dkey_heads.reshape(row_count, ATT), dvalue_heads.reshape(row_count, ATT)], axis=1
        ),
    )


def depthwise(extended, conv_kernel, row_count, ahead):
    tap_count = conv_kernel.shape[0]

    def add_tap(tap_index, running):
        first_row = tap_index if ahead else tap_count - 1 - tap_index
        return running + conv_kernel[tap_index] * lax.dynamic_slice_in_dim(
            extended, first_row, row_count, 0
        )

    empty = jnp.zeros((row_count, extended.shape[1]), jnp.float32)
    return lax.fori_loop(0, tap_count, add_tap, empty)


def sum_weights(weight_part, kernel_part):
    return lax.psum((weight_part, kernel_part), ("dp", "blk"))


def per_device(queries, key_in, value_in, out_weight, conv_kernel, cotangent):
    cycle_count = lax.axis_size("blk")
    device = lax.axis_index("blk")
    row_count = queries.shape[1]
    context = min(CTX_MAX, cycle_count // 4)
    left_span = context * row_count
    score_scale = 1.0 / math.sqrt(HEAD_DIM)
    edge_rows = conv_kernel.shape[0] - 1
    row_ids = jnp.arange(row_count, dtype=jnp.int32)
    query_heads = split_heads(queries[0])
    own_tile = jnp.concatenate([key_in[0], value_in[0]], axis=1)
    own_pos = device * row_count + row_ids
    always = jnp.array(True)

    def source(offset):
        anchor = device - offset
        return (anchor * row_count + row_ids, anchor >= 0)

    start_state = (
        jnp.full((ATT_HEADS, row_count), NEGATIVE, jnp.float32),
        jnp.zeros((ATT_HEADS, row_count), jnp.float32),
        jnp.zeros((row_count, ATT_HEADS, HEAD_DIM), jnp.float32),
    )
    first_state = attend_tile(
        start_state, query_heads, own_tile, own_pos, own_pos, always, left_span, score_scale
    )

    def forward_step(carry, offset):
        moving, softmax_state = carry
        arrived = from_behind(moving, "blk", 1)
        tile_pos, tile_usable = source(offset)
        softmax_state = attend_tile(
            softmax_state,
            query_heads,
            arrived,
            own_pos,
            tile_pos,
            tile_usable,
            left_span,
            score_scale,
        )
        return ((arrived, softmax_state), arrived)

    offsets = jnp.arange(1, context + 1, dtype=jnp.int32)
    (unused_tile, final_state), kept_tiles = lax.scan(
        forward_step, (own_tile, first_state), offsets
    )
    running_max, running_sum, weighted = final_state
    attended = (weighted / jnp.transpose(running_sum)[:, :, None]).astype(jnp.bfloat16)
    log_sums = running_max + jnp.log(running_sum)
    flat = attended.reshape(row_count, ATT)
    hidden = jnp.dot(flat, out_weight, preferred_element_type=jnp.float32).astype(jnp.bfloat16)
    before = from_behind(hidden[-edge_rows:], "blk", 1)
    extended = jnp.concatenate([before, hidden], axis=0).astype(jnp.float32)
    mixed = depthwise(extended, conv_kernel, row_count, False)
    sigma = jax.nn.sigmoid(mixed)
    out_frames = (mixed * sigma).astype(jnp.bfloat16)[None]
    upstream = cotangent[0].astype(jnp.float32)
    dmixed = upstream * sigma * (1.0 + mixed * (1.0 - sigma))
    after = from_behind(dmixed[:edge_rows].astype(jnp.bfloat16), "blk", -1).astype(jnp.float32)
    dextended = jnp.concatenate([dmixed, after], axis=0)
    dhidden = depthwise(dextended, conv_kernel, row_count, True).astype(jnp.bfloat16)

    def kernel_tap(tap_index):
        window = lax.dynamic_slice_in_dim(extended, edge_rows - tap_index, row_count, 0)
        return jnp.sum(dmixed * window, axis=0)

    kernel_part = lax.map(kernel_tap, jnp.arange(edge_rows + 1, dtype=jnp.int32))
    weight_part = jnp.einsum("ra,rd->ad", flat, dhidden, preferred_element_type=jnp.float32)
    dattended = jnp.einsum(
        "rd,ad->ra", dhidden, out_weight, preferred_element_type=jnp.float32
    ).astype(jnp.bfloat16)
    dout_heads = split_heads(dattended)
    deltas = jnp.einsum("rhe,rhe->hr", dout_heads, attended, preferred_element_type=jnp.float32)
    dquery_own, dkv_own = tile_grads(
        query_heads,
        dout_heads,
        log_sums,
        deltas,
        own_tile,
        own_pos,
        own_pos,
        always,
        left_span,
        score_scale,
    )
    zero_buffer = jnp.zeros((row_count, 2 * ATT), jnp.float32)

    def backward_step(carry, inputs):
        buffer, dquery_sum = carry
        tile, offset = inputs
        tile_pos, tile_usable = source(offset)
        dquery_part, dkv_part = tile_grads(
            query_heads,
            dout_heads,
            log_sums,
            deltas,
            tile,
            own_pos,
            tile_pos,
            tile_usable,
            left_span,
            score_scale,
        )
        arrived = from_behind((buffer + dkv_part).astype(jnp.bfloat16), "blk", -1).astype(
            jnp.float32
        )
        return ((arrived, dquery_sum + dquery_part), None)

    (buffer, dquery_sum), unused = lax.scan(
        backward_step, (zero_buffer, dquery_own), (kept_tiles, offsets), reverse=True
    )
    dkv_total = dkv_own + buffer
    weight_total, kernel_total = sum_weights(weight_part, kernel_part)
    query_grad = dquery_sum.reshape(row_count, ATT).astype(jnp.bfloat16)[None]
    key_grad = dkv_total[:, :ATT].astype(jnp.bfloat16)[None]
    value_grad = dkv_total[:, ATT:].astype(jnp.bfloat16)[None]
    return (out_frames, query_grad, key_grad, value_grad, weight_total, kernel_total)


def solution(mesh):
    return jax.shard_map(
        per_device,
        mesh=mesh,
        in_specs=(
            P("dp", "blk", None),
            P("dp", "blk", None),
            P("dp", "blk", None),
            P(),
            P(),
            P("dp", "blk", None),
        ),
        out_specs=(
            P("dp", "blk", None),
            P("dp", "blk", None),
            P("dp", "blk", None),
            P("dp", "blk", None),
            P(),
            P(),
        ),
        check_vma=False,
    )
```

profile of v0, /device:TPU:24, one launch (start us, length us, event | category | flops | bytes accessed | tf_op | source)
XLA Modules:
  0.0 622.3 jit_solution(3382806898935224929)
XLA Ops:
  12.4 69.9 %while.79 = (s32[]{:T(128)}, bf16[192,1024]{0,1:T(8,128)(2,1)S(1)}, f32[8,192]{1,0:T(8,128)S(1)}, f32[8,192]{1,0:T(8,128)S(1)}, f32[192,8,64]{0,2,1:T(8,128)S(1)...) while((s32[]{:T(128)}, bf16[192,1024]{0,1:T(8,128)(2,1)S(1)}, ...), condition=%wide.region_5.6_spmd.clone, body=%wide.region_2.5_spmd.clone.sunk | while | flops 78537600 | bytes 9227495 | solution.py:158
  12.4 4.9 collective-permute-start
  18.7 18.9 %collective-permute-done = bf16[192,1024]{0,1:T(8,128)(2,1)S(1)} collective-permute-done((bf16[192,1024]{0,1:T(8,128)(2,1)S(1)}, bf16[192,1024]{0,1:T(8,128)(2,1)S(1)}, u32[]{:S(2)}, u32[]{:S(2)}) %collective-permute-start) | collective-permute-done | bytes 393248 | tf_op jit(solution)/shard_map/while/body/eval_jaxpr/ppermute | solution.py:17
  39.8 1.9 collective-permute-start
  43.1 16.2 %collective-permute-done = bf16[192,1024]{0,1:T(8,128)(2,1)S(1)} collective-permute-done((bf16[192,1024]{0,1:T(8,128)(2,1)S(1)}, bf16[192,1024]{0,1:T(8,128)(2,1)S(1)}, u32[]{:S(2)}, u32[]{:S(2)}) %collective-permute-start) | collective-permute-done | bytes 393248 | tf_op jit(solution)/shard_map/while/body/eval_jaxpr/ppermute | solution.py:17
  61.5 1.9 collective-permute-start
  64.8 15.3 %collective-permute-done = bf16[192,1024]{0,1:T(8,128)(2,1)S(1)} collective-permute-done((bf16[192,1024]{0,1:T(8,128)(2,1)S(1)}, bf16[192,1024]{0,1:T(8,128)(2,1)S(1)}, u32[]{:S(2)}, u32[]{:S(2)}) %collective-permute-start) | collective-permute-done | bytes 393248 | tf_op jit(solution)/shard_map/while/body/eval_jaxpr/ppermute | solution.py:17
  82.8 1.9 collective-permute-start.2
  84.9 8.7 %collective-permute-done.2 = bf16[30,1024]{1,0:T(8,128)(2,1)S(1)} collective-permute-done((bf16[30,1024]{1,0:T(8,128)(2,1)S(1)}, bf16[30,1024]{1,0:T(8,128)(2,1)S(1)}, u32[]{:S(2)}, u32[]{:S(2)}) %collective-permute-start.2) | collective-permute-done | bytes 61472 | tf_op jit(solution)/shard_map/ppermute | solution.py:17
  94.6 36.2 %while.80 = (s32[]{:T(128)}, f32[192,1024]{1,0:T(8,128)S(1)}, f32[31,1024]{1,0:T(8,128)}, f32[222,1024]{1,0:T(8,128)S(1)}, s32[]{:T(128)}, /*index=5*/s32[]{:T(128)}, s32[]{:T(128)}, s32[]{:T(128)}) while((s32[]{:T(128)}, f32[192,1024]{1,0:T(8,128)S(1)}, f32[31,1024]{1,0:T(8,128)}, f32[222,1024]{1,0:T(8,128)S(1)}, s32[]{:T(128)}, ...), condition=%wide.region_7.8_spmd.clone, body=%wide.region_6.7_spmd.clone.sunk | while | flops 589831 | bytes 2371741 | solution.py:107
  131.7 2.3 fusion.39
  134.1 1.9 collective-permute-start.3
  136.0 106.3 %while.78 = (s32[]{:T(128)}, f32[31,1024]{1,0:T(8,128)}, s32[31]{0:T(128)S(1)}, f32[222,1024]{1,0:T(8,128)S(1)}, f32[192,1024]{1,0:T(8,128)S(1)}, /*index=5*/s32[]{:T(128)}, s32[1]{0:T(128)}, s32[]{:T(128)}, s32[1]{0:T(128)}) while((s32[]{:T(128)}, f32[31,1024]{1,0:T(8,128)}, s32[31]{0:T(128)S(1)}, f32[222,1024]{1,0:T(8,128)S(1)}, ...), condition=%wide.region_15.16_spmd, body=%wide.region_13.15_spmd.sunk | while | flops 392198 | bytes 1585319 | solution.py:181
  243.8 71.2 %while.81 = (s32[]{:T(128)}, f32[192,1024]{1,0:T(8,128)S(1)}, f32[31,1024]{1,0:T(8,128)}, f32[222,1024]{1,0:T(8,128)}, s32[]{:T(128)}, /*index=5*/s32[]{:T(128)}) while((s32[]{:T(128)}, f32[192,1024]{1,0:T(8,128)S(1)}, f32[31,1024]{1,0:T(8,128)}, f32[222,1024]{1,0:T(8,128)}, s32[]{:T(128)}, /*index=5*/s32[]{:T(128)}) %tuple.190), condition=%wide.region_9.10_spmd.clone, body=%wide.region_8.9_spmd.clone.sunk | while | flops 589827 | bytes 2371679 | solution.py:107
  244.6 1.5 select_add_fusion.5
  246.9 1.5 select_add_fusion.5
  249.2 1.5 select_add_fusion.5
  251.5 1.5 select_add_fusion.5
  253.8 1.5 select_add_fusion.5
  256.1 1.5 select_add_fusion.5
  258.4 1.5 select_add_fusion.5
  260.7 1.5 select_add_fusion.5
  263.0 1.5 select_add_fusion.5
  265.2 1.5 select_add_fusion.5
  267.5 1.5 select_add_fusion.5
  269.8 1.5 select_add_fusion.5
  279.0 1.5 select_add_fusion.5
  281.3 1.5 select_add_fusion.5
  288.2 1.5 select_add_fusion.5
  290.5 1.5 select_add_fusion.5
  299.7 1.5 select_add_fusion.5
  302.0 1.5 select_add_fusion.5
  311.2 1.5 select_add_fusion.5
  313.5 1.5 select_add_fusion.5
  315.9 2.4 convolution_convert_fusion.1
  324.2 1.8 fusion.48
  328.3 63.4 %while.82 = (s32[]{:T(128)}, f32[192,1024]{0,1:T(8,128)S(1)}, f32[192,8,64]{0,2,1:T(8,128)}, s32[3]{0:T(128)S(1)}, s32[]{:T(128)}, /*index=5*/bf16[3,192,1024]{1...) while((s32[]{:T(128)}, f32[192,1024]{0,1:T(8,128)S(1)}, ...), condition=%wide.region_11.12_spmd.clone, body=%wide.region_10.11_spmd.clone.sunk | while | flops 192565632 | bytes 15424801 | solution.py:223
  333.5 1.9 collective-permute-start.1
  335.4 2.2 fusion.139
  337.6 10.0 %collective-permute-done.1 = bf16[192,1024]{0,1:T(8,128)(2,1)} collective-permute-done((bf16[192,1024]{0,1:T(8,128)(2,1)}, bf16[192,1024]{0,1:T(8,128)(2,1)}, u32[]{:S(2)}, u32[]{:S(2)}) %collective-permute-start.1) | collective-permute-done | bytes 393248 | tf_op jit(solution)/shard_map/while/body/eval_jaxpr/ppermute | solution.py:17
  354.1 5.3 collective-permute-start.1
  359.4 2.2 fusion.139
  361.6 6.5 %collective-permute-done.1 = bf16[192,1024]{0,1:T(8,128)(2,1)} collective-permute-done((bf16[192,1024]{0,1:T(8,128)(2,1)}, bf16[192,1024]{0,1:T(8,128)(2,1)}, u32[]{:S(2)}, u32[]{:S(2)}) %collective-permute-start.1) | collective-permute-done | bytes 393248 | tf_op jit(solution)/shard_map/while/body/eval_jaxpr/ppermute | solution.py:17
  374.5 8.4 %collective-permute-start.1 = (bf16[192,1024]{0,1:T(8,128)(2,1)}, bf16[192,1024]{0,1:T(8,128)(2,1)}, u32[]{:S(2)}, u32[]{:S(2)}) collective-permute-start(bf16[192,1024]{0,1:T(8,128)(2,1)} %fusion.138), channel_id=1, source_target_pairs={{1,0},{2,1},{3,2},{4,3},{5,4},{6,5},{7,6},{8,7},{9,8},{10,9},{11,1... | collective-permute-start | bytes 1179656 | tf_op jit(solution)/shard_map/while/body/eval_jaxpr/ppermute | solution.py:17
  382.9 2.2 fusion.139
  385.1 5.4 collective-permute-done.1
  395.8 215.8 %all-reduce.3.cloned.1.call-done = (f32[512,1024]{1,0:T(8,128)}, f32[31,1024]{1,0:T(8,128)}) async-done(((f32[512,1024]{1,0:T(8,128)}, f32[31,1024]{1,0:T(8,128)}), (f32[512,1024]{1,0:T(8,128)}, f32[31,1024]{1,0:T(8,128)})) %all-reduce.3.cloned.1.call-update) | async-done | bytes 2224144 | tf_op jit(solution)/shard_map/psum | solution.py:111
  611.6 3.2 copy.121
  (347 shorter events, 190.2 us)
Async XLA Ops:
  7.2 75.2 %copy-start = (bf16[512,1024]{1,0:T(8,128)(2,1)S(1)}, bf16[512,1024]{1,0:T(8,128)(2,1)}, u32[]{:S(2)}) copy-start(bf16[512,1024]{1,0:T(8,128)(2,1)} %param.19) | copy-start | bytes 3145732
  7.2 604.5 %all-reduce.3.cloned.1.call-start = ((), (), s32[]{:S(2)}) async-start(), calls=%async_computation | async-start | bytes 4456448 | tf_op jit(solution)/shard_map/psum | solution.py:111
  8.6 3.1 copy-start.10
  11.3 1.1 copy-start.1
  12.4 25.2 %collective-permute-start = (bf16[192,1024]{0,1:T(8,128)(2,1)S(1)}, bf16[192,1024]{0,1:T(8,128)(2,1)S(1)}, u32[]{:S(2)}, u32[]{:S(2)}) collective-permute-start(bf16[192,1024]{0,1:T(8,128)(2,1)S(1)} %get-tuple-element.1015), channel_id=1, source_target_pairs={{0,1},{1,2},{2,3},{3,4},{4,5},{5,6},{6,7},{7,8},{8,9},{9,10},{10,1... | collective-permute-start | bytes 1179656 | tf_op jit(solution)/shard_map/while/body/eval_jaxpr/ppermute | solution.py:17
  39.8 19.5 %collective-permute-start = (bf16[192,1024]{0,1:T(8,128)(2,1)S(1)}, bf16[192,1024]{0,1:T(8,128)(2,1)S(1)}, u32[]{:S(2)}, u32[]{:S(2)}) collective-permute-start(bf16[192,1024]{0,1:T(8,128)(2,1)S(1)} %get-tuple-element.1015), channel_id=1, source_target_pairs={{0,1},{1,2},{2,3},{3,4},{4,5},{5,6},{6,7},{7,8},{8,9},{9,10},{10,1... | collective-permute-start | bytes 1179656 | tf_op jit(solution)/shard_map/while/body/eval_jaxpr/ppermute | solution.py:17
  61.5 18.6 %collective-permute-start = (bf16[192,1024]{0,1:T(8,128)(2,1)S(1)}, bf16[192,1024]{0,1:T(8,128)(2,1)S(1)}, u32[]{:S(2)}, u32[]{:S(2)}) collective-permute-start(bf16[192,1024]{0,1:T(8,128)(2,1)S(1)} %get-tuple-element.1015), channel_id=1, source_target_pairs={{0,1},{1,2},{2,3},{3,4},{4,5},{5,6},{6,7},{7,8},{8,9},{9,10},{10,1... | collective-permute-start | bytes 1179656 | tf_op jit(solution)/shard_map/while/body/eval_jaxpr/ppermute | solution.py:17
  82.3 2.5 copy-start.7
  82.4 2.5 copy-start.12
  82.8 2.0 copy-start.15
  82.8 10.7 %collective-permute-start.2 = (bf16[30,1024]{1,0:T(8,128)(2,1)S(1)}, bf16[30,1024]{1,0:T(8,128)(2,1)S(1)}, u32[]{:S(2)}, u32[]{:S(2)}) collective-permute-start(bf16[30,1024]{1,0:T(8,128)(2,1)S(1)} %slice.52), channel_id=1, source_target_pairs={{0,1},{1,2},{2,3},{3,4},{4,5},{5,6},{6,7},{7,8},{8,9},{9,10},{10,1... | collective-permute-start | bytes 184328 | tf_op jit(solution)/shard_map/ppermute | solution.py:17
  130.9 0.9 copy-start.8
  134.1 108.3 %collective-permute-start.3 = (bf16[30,1024]{1,0:T(8,128)(2,1)S(1)}, bf16[30,1024]{1,0:T(8,128)(2,1)S(1)}, u32[]{:S(2)}, u32[]{:S(2)}) collective-permute-start(bf16[30,1024]{1,0:T(8,128)(2,1)S(1)} %slice.59), channel_id=1, source_target_pairs={{1,0},{2,1},{3,2},{4,3},{5,4},{6,5},{7,6},{8,7},{9,8},{10,9},{11,1... | collective-permute-start | bytes 184328 | tf_op jit(solution)/shard_map/ppermute | solution.py:17
  242.4 1.5 copy-start.3
  315.0 0.9 copy-start.4
  315.9 4.6 copy-start.2
  321.8 0.9 copy-start.11
  322.7 1.4 copy-start.5
  322.7 1.4 copy-start.13
  324.2 1.8 copy-start.14
  326.9 1.4 copy-start.6
  330.6 0.8 copy-start.9
  333.5 14.1 %collective-permute-start.1 = (bf16[192,1024]{0,1:T(8,128)(2,1)}, bf16[192,1024]{0,1:T(8,128)(2,1)}, u32[]{:S(2)}, u32[]{:S(2)}) collective-permute-start(bf16[192,1024]{0,1:T(8,128)(2,1)} %fusion.138), channel_id=1, source_target_pairs={{1,0},{2,1},{3,2},{4,3},{5,4},{6,5},{7,6},{8,7},{9,8},{10,9},{11,1... | collective-permute-start | bytes 1179656 | tf_op jit(solution)/shard_map/while/body/eval_jaxpr/ppermute | solution.py:17
  351.2 0.8 copy-start.9
  354.1 14.0 %collective-permute-start.1 = (bf16[192,1024]{0,1:T(8,128)(2,1)}, bf16[192,1024]{0,1:T(8,128)(2,1)}, u32[]{:S(2)}, u32[]{:S(2)}) collective-permute-start(bf16[192,1024]{0,1:T(8,128)(2,1)} %fusion.138), channel_id=1, source_target_pairs={{1,0},{2,1},{3,2},{4,3},{5,4},{6,5},{7,6},{8,7},{9,8},{10,9},{11,1... | collective-permute-start | bytes 1179656 | tf_op jit(solution)/shard_map/while/body/eval_jaxpr/ppermute | solution.py:17
  371.6 0.8 copy-start.9
  374.5 16.0 %collective-permute-start.1 = (bf16[192,1024]{0,1:T(8,128)(2,1)}, bf16[192,1024]{0,1:T(8,128)(2,1)}, u32[]{:S(2)}, u32[]{:S(2)}) collective-permute-start(bf16[192,1024]{0,1:T(8,128)(2,1)} %fusion.138), channel_id=1, source_target_pairs={{1,0},{2,1},{3,2},{4,3},{5,4},{6,5},{7,6},{8,7},{9,8},{10,9},{11,1... | collective-permute-start | bytes 1179656 | tf_op jit(solution)/shard_map/while/body/eval_jaxpr/ppermute | solution.py:17
  611.6 3.2 copy-start.16
Sparse Core Ops, SparseCore 0:
  328.0 283.6 all-reduce.2
where the time goes:
time: 632 us; the launch traced here: 622 us
  waiting for transfers between devices  297 us (47%)
  local copies, waits for them, and re-layouts  134 us (21%)
  other arithmetic  79.2 us (13%)
  loops' own time  46.3 us (7%)
  starting transfers between devices  28.2 us (4%)
  matrix products  23.3 us (4%)
  between operations  14.4 us (2%)
    psum x1, waiting for transfers between devices, sum_weights(): return lax.psum((weight_part, kernel_part), ('dp', 'blk'))  216 us
    ppermute x8, waiting for transfers between devices, from_behind(): return lax.ppermute(block, axis, route)  81.1 us
    add x62, other arithmetic, add_tap(): running + conv_kernel[tap_index] * lax.dynamic_slice_in_dim(extended, fir...  58.3 us
    dynamic_slice x62, local copies, waits for them, and re-layouts, add_tap(): conv_kernel[tap_index]  47.7 us
    dynamic_update_slice x31, local copies, waits for them, and re-layouts, per_device(): lax.map(kernel_tap, jnp.arange(edge_rows + 1, dtype=jnp.int32))  43.4 us
    another operation x1, loops' own time, per_device(): lax.map(kernel_tap, jnp.arange(edge_rows + 1, dtype=jnp.int32))  40.4 us
    ppermute x8, starting transfers between devices, from_behind(): return lax.ppermute(block, axis, route)  28.1 us
    dynamic_slice x31, local copies, waits for them, and re-layouts, per_device(): lax.map(kernel_tap, jnp.arange(edge_rows + 1, dtype=jnp.int32))  18 us
  transfers between devices with their start and end apart: 9, of which 8 were waited for; matrix products, arithmetic and copies ran while one was open for 15% of the time, Pallas kernels for 0%

commit v1 on v0

--- a/solution.py
+++ b/solution.py
@@ -3,6 +3,7 @@
 import jax.numpy as jnp
 from jax import lax
 from jax.sharding import PartitionSpec as P
+from jax.lax import psum
 
 ATT_HEADS = 8
 HEAD_DIM = 64
@@ -108,7 +109,12 @@
 
 
 def sum_weights(weight_part, kernel_part):
-    return lax.psum((weight_part, kernel_part), ("dp", "blk"))
+
+    def cubes_handle(block_here, chip_axis, group_axis):
+        current_block = psum(block_here, axis_name=chip_axis)
+        return psum(current_block, axis_name=group_axis)
+
+    return cubes_handle((weight_part, kernel_part), "blk", "dp")
 
 
 def per_device(queries, key_in, value_in, out_weight, conv_kernel, cotangent):

time: 632 us -> 1740 us (2.75)
  the two profiles are of different devices: /device:TPU:24 before, /device:TPU:11 now
where the time goes in v1:
time: 1740 us
  waiting for transfers between devices  1410 us (81%)
  local copies, waits for them, and re-layouts  134 us (8%)
  other arithmetic  79.1 us (5%)
  loops' own time  46.3 us (3%)
  starting transfers between devices  30.2 us (2%)
  matrix products  24.4 us (1%)
    psum x1, waiting for transfers between devices, cubes_handle(): current_block = psum(block_here, axis_name=chip_axis)  1240 us
    psum x1, waiting for transfers between devices, cubes_handle(): return psum(current_block, axis_name=group_axis)  99.2 us
    ppermute x8, waiting for transfers between devices, from_behind(): return lax.ppermute(block, axis, route)  70.9 us
    add x62, other arithmetic, add_tap(): running + conv_kernel[tap_index] * lax.dynamic_slice_in_dim(extended, fir...  58.3 us
    dynamic_slice x62, local copies, waits for them, and re-layouts, add_tap(): conv_kernel[tap_index]  47.7 us
    dynamic_update_slice x31, local copies, waits for them, and re-layouts, per_device(): lax.map(kernel_tap, jnp.arange(edge_rows + 1, dtype=jnp.int32))  43.4 us
    another operation x1, loops' own time, per_device(): lax.map(kernel_tap, jnp.arange(edge_rows + 1, dtype=jnp.int32))  40.4 us
  transfers between devices with their start and end apart: 10, of which 9 were waited for; matrix products, arithmetic and copies ran while one was open for 6% of the time, Pallas kernels for 0%

profile of v1, /device:TPU:11, one launch (start us, length us, event | category | flops | bytes accessed | tf_op | source)
XLA Modules:
  0.0 1735.5 jit_solution(4325754507855716979)
XLA Ops:
  12.4 66.6 %while.79 = (s32[]{:T(128)}, bf16[192,1024]{0,1:T(8,128)(2,1)S(1)}, f32[8,192]{1,0:T(8,128)S(1)}, f32[8,192]{1,0:T(8,128)S(1)}, f32[192,8,64]{0,2,1:T(8,128)S(1)...) while((s32[]{:T(128)}, bf16[192,1024]{0,1:T(8,128)(2,1)S(1)}, ...), condition=%wide.region_5.6_spmd.clone, body=%wide.region_2.5_spmd.clone.sunk | while | flops 78537600 | bytes 9227495 | solution.py:164
  12.4 3.7 collective-permute-start
  17.5 18.6 %collective-permute-done = bf16[192,1024]{0,1:T(8,128)(2,1)S(1)} collective-permute-done((bf16[192,1024]{0,1:T(8,128)(2,1)S(1)}, bf16[192,1024]{0,1:T(8,128)(2,1)S(1)}, u32[]{:S(2)}, u32[]{:S(2)}) %collective-permute-start) | collective-permute-done | bytes 393248 | tf_op jit(solution)/shard_map/while/body/eval_jaxpr/ppermute | solution.py:18
  38.3 1.9 collective-permute-start
  41.6 15.3 collective-permute-done
  59.1 1.9 collective-permute-start
  62.4 14.3 collective-permute-done
  79.5 1.9 collective-permute-start.2
  81.5 7.5 collective-permute-done.2
  90.1 36.2 %while.80 = (s32[]{:T(128)}, f32[192,1024]{1,0:T(8,128)S(1)}, f32[31,1024]{1,0:T(8,128)}, f32[222,1024]{1,0:T(8,128)S(1)}, s32[]{:T(128)}, /*index=5*/s32[]{:T(128)}, s32[]{:T(128)}, s32[]{:T(128)}) while((s32[]{:T(128)}, f32[192,1024]{1,0:T(8,128)S(1)}, f32[31,1024]{1,0:T(8,128)}, f32[222,1024]{1,0:T(8,128)S(1)}, s32[]{:T(128)}, ...), condition=%wide.region_7.8_spmd.clone, body=%wide.region_6.7_spmd.clone.sunk | while | flops 589831 | bytes 2371741 | solution.py:108
  127.2 2.3 fusion.39
  129.6 1.9 collective-permute-start.3
  131.5 106.3 %while.78 = (s32[]{:T(128)}, f32[31,1024]{1,0:T(8,128)}, s32[31]{0:T(128)S(1)}, f32[222,1024]{1,0:T(8,128)S(1)}, f32[192,1024]{1,0:T(8,128)S(1)}, /*index=5*/s32[]{:T(128)}, s32[1]{0:T(128)}, s32[]{:T(128)}, s32[1]{0:T(128)}) while((s32[]{:T(128)}, f32[31,1024]{1,0:T(8,128)}, s32[31]{0:T(128)S(1)}, f32[222,1024]{1,0:T(8,128)S(1)}, ...), condition=%wide.region_16.17_spmd, body=%wide.region_14.16_spmd.sunk | while | flops 392198 | bytes 1585319 | solution.py:187
  239.3 71.2 %while.81 = (s32[]{:T(128)}, f32[192,1024]{1,0:T(8,128)S(1)}, f32[31,1024]{1,0:T(8,128)}, f32[222,1024]{1,0:T(8,128)}, s32[]{:T(128)}, /*index=5*/s32[]{:T(128)}) while((s32[]{:T(128)}, f32[192,1024]{1,0:T(8,128)S(1)}, f32[31,1024]{1,0:T(8,128)}, f32[222,1024]{1,0:T(8,128)}, s32[]{:T(128)}, /*index=5*/s32[]{:T(128)}) %tuple.193), condition=%wide.region_9.10_spmd.clone, body=%wide.region_8.9_spmd.clone.sunk | while | flops 589827 | bytes 2371679 | solution.py:108
  240.1 1.5 select_add_fusion.5
  242.4 1.5 select_add_fusion.5
  244.7 1.5 select_add_fusion.5
  247.0 1.5 select_add_fusion.5
  249.3 1.5 select_add_fusion.5
  251.6 1.5 select_add_fusion.5
  253.9 1.5 select_add_fusion.5
  260.8 1.5 select_add_fusion.5
  263.1 1.5 select_add_fusion.5
  272.2 1.5 select_add_fusion.5
  274.5 1.5 select_add_fusion.5
  283.7 1.5 select_add_fusion.5
  286.0 1.5 select_add_fusion.5
  292.9 1.5 select_add_fusion.5
  295.2 1.5 select_add_fusion.5
  304.4 1.5 select_add_fusion.5
  306.7 1.5 select_add_fusion.5
  310.5 1.8 fusion.48
  312.4 2.4 convolution_convert_fusion.1
  317.1 2.0 copy.51
  323.0 2.3 fusion.33
  325.3 1236.3 %all-reduce.5.cloned.1.call-done = (f32[512,1024]{1,0:T(8,128)}, f32[31,1024]{1,0:T(8,128)}) async-done(((f32[512,1024]{1,0:T(8,128)}, f32[31,1024]{1,0:T(8,128)}), (f32[512,1024]{1,0:T(8,128)}, f32[31,1024]{1,0:T(8,128)})) %all-reduce.5.cloned.1.call-update) | async-done | bytes 2224144 | tf_op jit(solution)/shard_map/psum | solution.py:114
  1561.7 59.7 %while.82 = (s32[]{:T(128)}, f32[192,1024]{0,1:T(8,128)S(1)}, f32[192,8,64]{0,2,1:T(8,128)}, s32[3]{0:T(128)S(1)}, s32[]{:T(128)}, /*index=5*/bf16[3,192,1024]{1...) while((s32[]{:T(128)}, f32[192,1024]{0,1:T(8,128)S(1)}, ...), condition=%wide.region_11.12_spmd.clone, body=%wide.region_10.11_spmd.clone.sunk | while | flops 192565632 | bytes 15424801 | solution.py:229
  1567.0 3.9 collective-permute-start.1
  1570.8 2.2 fusion.139
  1573.0 6.3 collective-permute-done.1
  1585.7 6.5 collective-permute-start.1
  1592.3 2.2 fusion.139
  1594.5 4.5 collective-permute-done.1
  1605.3 8.4 collective-permute-start.1
  1613.7 2.2 fusion.139
  1615.9 4.3 collective-permute-done.1
  1625.6 99.2 %all-reduce.7.cloned.1.call-done = (f32[512,1024]{1,0:T(8,128)}, f32[31,1024]{1,0:T(8,128)}) async-done(((f32[512,1024]{1,0:T(8,128)}, f32[31,1024]{1,0:T(8,128)}), (f32[512,1024]{1,0:T(8,128)}, f32[31,1024]{1,0:T(8,128)})) %all-reduce.7.cloned.1.call-update) | async-done | bytes 2224144 | tf_op jit(solution)/shard_map/psum | solution.py:115
  1724.8 3.2 copy.123
  (348 shorter events, 192.0 us)
Async XLA Ops:
  7.2 71.9 %copy-start = (bf16[512,1024]{1,0:T(8,128)(2,1)S(1)}, bf16[512,1024]{1,0:T(8,128)(2,1)}, u32[]{:S(2)}) copy-start(bf16[512,1024]{1,0:T(8,128)(2,1)} %param.19) | copy-start | bytes 3145732
  7.2 1554.4 %all-reduce.5.cloned.1.call-start = ((), (), s32[]{:S(2)}) async-start(), calls=%async_computation | async-start | bytes 4456448 | tf_op jit(solution)/shard_map/psum | solution.py:114
  8.6 3.1 copy-start.10
  11.3 1.1 copy-start.1
  12.4 23.7 %collective-permute-start = (bf16[192,1024]{0,1:T(8,128)(2,1)S(1)}, bf16[192,1024]{0,1:T(8,128)(2,1)S(1)}, u32[]{:S(2)}, u32[]{:S(2)}) collective-permute-start(bf16[192,1024]{0,1:T(8,128)(2,1)S(1)} %get-tuple-element.1017), channel_id=1, source_target_pairs={{0,1},{1,2},{2,3},{3,4},{4,5},{5,6},{6,7},{7,8},{8,9},{9,10},{10,1... | collective-permute-start | bytes 1179656 | tf_op jit(solution)/shard_map/while/body/eval_jaxpr/ppermute | solution.py:18
  38.3 18.6 %collective-permute-start = (bf16[192,1024]{0,1:T(8,128)(2,1)S(1)}, bf16[192,1024]{0,1:T(8,128)(2,1)S(1)}, u32[]{:S(2)}, u32[]{:S(2)}) collective-permute-start(bf16[192,1024]{0,1:T(8,128)(2,1)S(1)} %get-tuple-element.1017), channel_id=1, source_target_pairs={{0,1},{1,2},{2,3},{3,4},{4,5},{5,6},{6,7},{7,8},{8,9},{9,10},{10,1... | collective-permute-start | bytes 1179656 | tf_op jit(solution)/shard_map/while/body/eval_jaxpr/ppermute | solution.py:18
  59.1 17.6 %collective-permute-start = (bf16[192,1024]{0,1:T(8,128)(2,1)S(1)}, bf16[192,1024]{0,1:T(8,128)(2,1)S(1)}, u32[]{:S(2)}, u32[]{:S(2)}) collective-permute-start(bf16[192,1024]{0,1:T(8,128)(2,1)S(1)} %get-tuple-element.1017), channel_id=1, source_target_pairs={{0,1},{1,2},{2,3},{3,4},{4,5},{5,6},{6,7},{7,8},{8,9},{9,10},{10,1... | collective-permute-start | bytes 1179656 | tf_op jit(solution)/shard_map/while/body/eval_jaxpr/ppermute | solution.py:18
  79.0 2.5 copy-start.6
  79.0 2.4 copy-start.12
  79.5 2.0 copy-start.14
  79.5 9.5 collective-permute-start.2
  126.4 0.9 copy-start.7
  129.6 108.2 %collective-permute-start.3 = (bf16[30,1024]{1,0:T(8,128)(2,1)S(1)}, bf16[30,1024]{1,0:T(8,128)(2,1)S(1)}, u32[]{:S(2)}, u32[]{:S(2)}) collective-permute-start(bf16[30,1024]{1,0:T(8,128)(2,1)S(1)} %slice.59), channel_id=1, source_target_pairs={{1,0},{2,1},{3,2},{4,3},{5,4},{6,5},{7,6},{8,7},{9,8},{10,9},{11,1... | collective-permute-start | bytes 184328 | tf_op jit(solution)/shard_map/ppermute | solution.py:18
  237.8 1.5 copy-start.3
  239.3 71.2 %copy-start.13 = (bf16[192,8,64]{0,2,1:T(8,128)(2,1)S(1)}, bf16[192,8,64]{0,2,1:T(8,128)(2,1)}, u32[]{:S(2)}) copy-start(bf16[192,8,64]{0,2,1:T(8,128)(2,1)} %copy-done.12) | copy-start | bytes 589828
  310.5 1.8 copy-start.4
  312.3 3.6 copy-start.2
  312.3 1412.5 %all-reduce.7.cloned.1.call-start = ((), (), s32[]{:S(2)}) async-start(), calls=%async_computation.1 | async-start | bytes 4456448 | tf_op jit(solution)/shard_map/psum | solution.py:115
  320.8 0.9 copy-start.9
  321.7 1.4 copy-start.11
  323.0 1238.6 %copy-start.5 = (f32[192,1024]{0,1:T(8,128)S(1)}, f32[192,1024]{0,1:T(8,128)}, u32[]{:S(2)}) copy-start(f32[192,1024]{0,1:T(8,128)} %custom-call.2) | copy-start | bytes 2359300
  1564.0 0.8 copy-start.8
  1567.0 12.4 collective-permute-start.1
  1582.8 0.8 copy-start.8
  1585.7 13.2 collective-permute-start.1
  1602.4 0.8 copy-start.8
  1605.3 15.0 collective-permute-start.1
  1724.8 3.2 copy-start.15
Sparse Core Ops, SparseCore 0:
  312.4 1249.1 all-reduce.4
  1565.0 159.7 all-reduce.6
